TPU v7x, 32 devices: a whole 2x2x4 slice. The times are simulated.
32 devices in a mesh: seg: 8 (over z, x), space: 4 (over y, core).
Axes of the slice: x: 2, y: 2, z: 4, core: 2. Of those that a mesh axis runs over, the one named last changes fastest.
Arguments:
- states: float32 [8, 32, 65, 128], P('seg', 'space'), may hold values from -6 to 6
- forcing: float32 [32, 65, 128], P('space'), may hold values from -6 to 6
- wall_viscosity: float32 [65], replicated, may hold values from 0.5 to 4
Outputs:
- new_states: float32 [8, 32, 65, 128], P('seg', 'space')
- mismatch: float32 [8, 32, 65, 128], P('seg', 'space')
All inputs are finite; a program needn't handle non-finite values.
Results may differ from a plain program's by a relative error of at most 0.0075.
Values sent between devices are 32-bit elements; how exact they have to be, the bound alone decides.
No kernel may reach another device: no remote copies, remote signals or barrier semaphores. Data moves between devices by JAX's collectives and lax.ppermute only.
A program may use at most 64 MiB of HBM per device.

v0:
```python
import jax
import jax.numpy as jnp
from jax import lax
from jax.sharding import PartitionSpec as P

NY = 65
STEPS = 4
ITERS = 2
ADVECT = 0.15
SPREAD = 0.2
PUSHED = 0.25
EPSILON = 1e-06


def padded_2(shard, sides, width):
    for axis, dim in sides:
        devices, length = (lax.axis_size(axis), shard.shape[dim])
        up = [(i, (i + 1) % devices) for i in range(devices)]
        down = [(j, i) for i, j in up]
        last = lax.slice_in_dim(shard, length - width, length, axis=dim)
        initial = lax.slice_in_dim(shard, 0, width, axis=dim)
        before = lax.ppermute(last, axis, up)
        after = lax.ppermute(initial, axis, down)
        shard = jnp.concatenate([before, shard, after], axis=dim)
    return shard


def shifted(block, axis, distance):
    devices = range(lax.axis_size(axis))
    route = [((i - distance) % len(devices), i) for i in devices]
    return lax.ppermute(block, axis, route)


def inverses(viscosity):
    points = viscosity.shape[0]
    zero = jnp.zeros((1,), jnp.float32)
    negative = -viscosity
    centre = 1.0 + 2.0 * viscosity
    lower = jnp.concatenate([zero, negative[1:]])
    upper = jnp.concatenate([negative[:-1], zero])
    identity = jnp.eye(points, dtype=jnp.float32)
    return lax.linalg.tridiagonal_solve(lower[None], centre[None], upper[None], identity[None])[0]


def apply_inverse(inverse, field):
    return jnp.einsum("jk,xkz->xjz", inverse, field, precision=lax.Precision.HIGHEST)


def apply_transposed(inverse, field):
    return jnp.einsum("kj,xkz->xjz", inverse, field, precision=lax.Precision.HIGHEST)


def spanwise(field):
    return jnp.roll(field, 1, 2) + jnp.roll(field, -1, 2) - 2.0 * field


def forward_step(field, forcing, base, inverse):
    padded = padded_2(field, (("space", 0),), 1)
    slope = 0.5 * (padded[2:] - padded[:-2])
    pushed = field - ADVECT * (base + field) * slope + SPREAD * spanwise(field) + PUSHED * forcing
    return (apply_inverse(inverse, pushed), slope)


def adjoint_step(weight, field, slope, base, inverse):
    carried = apply_transposed(inverse, weight)
    flux = (base + field) * carried
    padded = padded_2(flux, (("space", 0),), 1)
    return (
        carried
        - ADVECT * carried * slope
        + ADVECT * (0.5 * (padded[2:] - padded[:-2]))
        + SPREAD * spanwise(carried)
    )


def integrate(field, forcing, base, inverse):
    saved = []
    for step in range(STEPS):
        following, slope = forward_step(field, forcing, base, inverse)
        saved.append((field, slope))
        field = following
    return (field, saved)


def adjoint(weight, saved, base, inverse):
    for step in reversed(range(len(saved))):
        weight = adjoint_step(weight, saved[step][0], saved[step][1], base, inverse)
    return weight


def per_device(states, forcing, wall_viscosity):
    current = states[0]
    base = (2.0 * jnp.arange(NY, dtype=jnp.float32) / (NY - 1) - 1.0)[None, :, None]
    inverse = inverses(wall_viscosity)
    mismatch = current
    for iteration in range(ITERS):
        ending, saved = integrate(current, forcing, base, inverse)
        prior = shifted(ending, "seg", 1)
        earlier = prior - current
        mismatch = shifted(earlier, "seg", -1)
        back = adjoint(mismatch, saved, base, inverse)
        descent = back - earlier
        total, squares = lax.psum(
            (0.5 * jnp.sum(mismatch * mismatch), jnp.sum(descent * descent)), ("seg", "space")
        )
        current = current - total / (squares + EPSILON) * descent
    return (current[None], mismatch[None])


def solution(mesh):
    placed = (P("seg", "space", None, None), P("space", None, None), P())
    return jax.shard_map(
        per_device,
        mesh=mesh,
        in_specs=placed,
        out_specs=(P("seg", "space", None, None), P("seg", "space", None, None)),
        check_vma=False,
    )
```

profile of v0, /device:TPU:0, one launch (start us, length us, event | category | flops | bytes accessed | tf_op | source)
XLA Modules:
  0.0 419.8 jit_solution(12235927826151954652)
XLA Ops:
  0.6 1.0 copy.69
  1.7 2.5 collective-permute-start
  5.8 170.1 %while.32 = (s32[]{:T(128)}, f32[1]{0:T(128)}, f32[1,65]{1,0:T(1,128)S(1)}, f32[2,32,1]{1,2,0:T(1,128)S(1)}, f32[2,32,1,65]{3,1,2,0:T(8,128)S(1)}, /*index=5*/f3...) while((s32[]{:T(128)}, f32[1]{0:T(128)}, ...), condition=%wide.region_1.2_spmd, body=%wide.region_0.1_spmd.sunk | while | flops 6369 | bytes 103045 | solution.py:42
  7.9 0.7 fusion.724
  8.6 0.7 fusion.726
  10.0 0.7 fusion.725
  73.4 0.7 constant_dynamic-update-slice_fusion.140
  92.9 0.7 fusion.724
  93.6 0.7 fusion.726
  95.1 0.7 fusion.725
  175.8 44.2 %while.33 = (s32[]{:T(128)}, f32[1,65]{1,0:T(1,128)S(1)}, f32[2,32,1,65]{3,1,2,0:T(8,128)S(1)}, f32[2,32,1,65]{3,2,1,0:T(1,128)S(1)}, f32[2,32,1]{1,2,0:T(1,128)...) while((s32[]{:T(128)}, f32[1,65]{1,0:T(1,128)S(1)}, ...), condition=%wide.region_3.4_spmd, body=%wide.region_2.3_spmd.sunk | while | flops 4193 | bytes 91485 | solution.py:42
  176.6 0.7 fusion.729
  177.3 19.5 %constant_dynamic-update-slice_fusion.168 = (f32[32,1,65]{2,1,0:T(1,128)S(1)}, f32[1,65]{1,0:T(1,128)S(1)}, f32[1,65]{1,0:T(1,128)S(1)}, f32[1,65]{1,0:T(1,128)S...) fusion(f32[]{:T(128)} %bitcast.1400, ...), kind=kLoop, calls=%fused_computation.196.clone.1 | loop fusion | flops 4029 | bytes 24956 | tf_op jit(solution)/shard_map/vmap()/while
  198.7 0.7 fusion.729
  199.4 19.5 %constant_dynamic-update-slice_fusion.168 = (f32[32,1,65]{2,1,0:T(1,128)S(1)}, f32[1,65]{1,0:T(1,128)S(1)}, f32[1,65]{1,0:T(1,128)S(1)}, f32[1,65]{1,0:T(1,128)S...) fusion(f32[]{:T(128)} %bitcast.1400, ...), kind=kLoop, calls=%fused_computation.196.clone.1 | loop fusion | flops 4029 | bytes 24956 | tf_op jit(solution)/shard_map/vmap()/while
  221.0 1.8 collective-permute-start.2
  222.9 1.7 collective-permute-done.2
  224.6 1.6 collective-permute-done.3
  227.9 1.5 collective-permute-done.4
  229.4 1.7 collective-permute-done.5
  232.7 1.3 collective-permute-done.6
  234.0 1.9 collective-permute-done.7
  235.8 1.5 convolution_bitcast_fusion.12
  237.3 1.6 collective-permute-start.8
  238.9 8.8 %collective-permute-done.8 = f32[8,65,128]{2,1,0:T(8,128)S(1)} collective-permute-done((f32[8,65,128]{2,1,0:T(8,128)S(1)}, f32[8,65,128]{2,1,0:T(8,128)S(1)}, u32[]{:S(2)}, u32[]{:S(2)}) %collective-permute-start.8) | collective-permute-done | bytes 266272 | tf_op jit(solution)/shard_map/ppermute | solution.py:31
  247.8 1.8 collective-permute-start.9
  249.6 5.0 %collective-permute-done.9 = f32[8,65,128]{2,1,0:T(8,128)S(1)} collective-permute-done((f32[8,65,128]{2,1,0:T(8,128)S(1)}, f32[8,65,128]{2,1,0:T(8,128)S(1)}, u32[]{:S(2)}, u32[]{:S(2)}) %collective-permute-start.9) | collective-permute-done | bytes 266272 | tf_op jit(solution)/shard_map/ppermute | solution.py:31
  255.2 0.9 fusion.694
  256.7 1.6 collective-permute-start.10
  259.5 0.8 collective-permute-done.10
  260.3 2.3 collective-permute-done.11
  262.5 1.7 add_multiply_fusion.5
  265.1 0.8 collective-permute-done.12
  266.0 2.0 collective-permute-done.13
  269.5 0.8 collective-permute-done.14
  270.3 2.0 collective-permute-done.15
  273.8 0.8 collective-permute-done.16
  274.7 2.0 collective-permute-done.17
  276.6 0.9 multiply_reduce_fusion.2
  277.5 40.1 %all-reduce.1 = (f32[]{:T(128)}, f32[]{:T(128)}) all-reduce(f32[]{:T(128)S(6)} %mul.1494, f32[]{:T(128)} %get-tuple-element.304), channel_id=1, replica_groups=mesh['seg'=8,'space'=4] {'seg','space'}, use_global_device_ids=true, to_apply=%region_5.6 | all-reduce | flops 2 | bytes 16 | tf_op jit(solution)/shard_map/psum | solution.py:103
  319.9 1.1 collective-permute-done.18
  321.0 2.7 collective-permute-done.19
  325.2 1.0 collective-permute-done.20
  326.2 2.0 collective-permute-done.21
  329.7 1.0 collective-permute-done.22
  330.7 2.0 collective-permute-done.23
  334.2 1.0 collective-permute-done.24
  335.2 2.0 collective-permute-done.25
  337.9 1.9 collective-permute-start.26
  339.8 9.8 %collective-permute-done.26 = f32[8,65,128]{2,1,0:T(8,128)S(1)} collective-permute-done((f32[8,65,128]{2,1,0:T(8,128)S(1)}, f32[8,65,128]{2,1,0:T(8,128)S(1)}, u32[]{:S(2)}, u32[]{:S(2)}) %collective-permute-start.26) | collective-permute-done | bytes 266272 | tf_op jit(solution)/shard_map/ppermute | solution.py:31
  349.8 8.2 %collective-permute-done.27 = f32[8,65,128]{2,1,0:T(8,128)S(1)} collective-permute-done((f32[8,65,128]{2,1,0:T(8,128)S(1)}, f32[8,65,128]{2,1,0:T(8,128)S(1)}, u32[]{:S(2)}, u32[]{:S(2)}) %collective-permute-start.27) | collective-permute-done | bytes 266272 | tf_op jit(solution)/shard_map/ppermute | solution.py:31
  358.5 0.9 fusion.670
  361.9 0.8 copy.22
  362.7 1.1 collective-permute-done.29
  363.7 1.4 add_multiply_fusion.1
  366.1 1.2 collective-permute-done.30
  367.3 1.7 collective-permute-done.31
  370.5 1.1 collective-permute-done.32
  371.6 1.7 collective-permute-done.33
  374.9 1.1 collective-permute-done.34
  376.0 1.7 collective-permute-done.35
  377.7 0.9 multiply_reduce_fusion
  378.6 39.1 %all-reduce = (f32[]{:T(128)}, f32[]{:T(128)}) all-reduce(f32[]{:T(128)S(6)} %mul.1544, f32[]{:T(128)} %get-tuple-element.302), channel_id=1, replica_groups=mesh['seg'=8,'space'=4] {'seg','space'}, use_global_device_ids=true, to_apply=%region_9.10 | all-reduce | flops 2 | bytes 16 | tf_op jit(solution)/shard_map/psum | solution.py:103
  419.0 0.8 copy.21
  (301 shorter events, 72.5 us)
Async XLA Ops:
  1.7 218.4 %collective-permute-start = (f32[1,65,128]{2,1,0:T(8,128)S(1)}, f32[1,65,128]{2,1,0:T(8,128)S(1)}, u32[]{:S(2)}, u32[]{:S(2)}) collective-permute-start(f32[1,65,128]{2,1,0:T(8,128)S(1)} %get-tuple-element.526), channel_id=1, source_target_pairs={{1,0},{2,1},{3,2},{0,3},{5,4},{6,5},{7,6},{4,7},{9,8},{10,9},{11,1... | collective-permute-start | bytes 99848 | tf_op jit(solution)/shard_map/ppermute | solution.py:23
  4.1 216.0 %collective-permute-start.1 = (f32[1,65,128]{2,1,0:T(8,128)S(1)}, f32[1,65,128]{2,1,0:T(8,128)S(1)}, u32[]{:S(2)}, u32[]{:S(2)}) collective-permute-start(f32[1,65,128]{2,1,0:T(8,128)S(1)} %get-tuple-element.527), channel_id=1, source_target_pairs={{0,1},{1,2},{2,3},{3,0},{4,5},{5,6},{6,7},{7,4},{8,9},{9,10},{10,1... | collective-permute-start | bytes 99848 | tf_op jit(solution)/shard_map/ppermute | solution.py:22
  4.3 0.7 copy-start.17
  175.8 44.3 %copy-start = (f32[8,65,128]{2,0,1:T(8,128)S(1)}, f32[8,65,128]{2,0,1:T(8,128)}, u32[]{:S(2)}) copy-start(f32[8,65,128]{2,0,1:T(8,128)} %param.8) | copy-start | bytes 798724
  220.1 0.7 copy-start.3
  220.1 0.7 copy-start.5
  221.0 3.6 collective-permute-start.2
  222.8 3.4 collective-permute-start.3
  224.6 2.3 copy-start.7
  226.1 0.7 copy-start.9
  227.0 2.4 collective-permute-start.4
  227.7 3.4 collective-permute-start.5
  229.4 2.4 copy-start.11
  231.1 0.7 copy-start.13
  232.0 2.0 collective-permute-start.6
  232.3 3.5 collective-permute-start.7
  235.8 11.9 %copy-start.1 = (f32[1,8,65,128]{3,1,2,0:T(8,128)S(1)}, f32[1,8,65,128]{3,1,2,0:T(8,128)}, u32[]{:S(2)}) copy-start(f32[1,8,65,128]{3,1,2,0:T(8,128)} %param.7) | copy-start | bytes 798724
  237.3 10.4 %collective-permute-start.8 = (f32[8,65,128]{2,1,0:T(8,128)S(1)}, f32[8,65,128]{2,1,0:T(8,128)S(1)}, u32[]{:S(2)}, u32[]{:S(2)}) collective-permute-start(f32[8,65,128]{2,1,0:T(8,128)S(1)} %convolution_bitcast_fusion.12), channel_id=1, source_target_pairs={{28,0},{0,4},{4,8},{8,12},{12,16},{16,20},{20,24},{24,28},{29,1},{... | collective-permute-start | bytes 798728 | tf_op jit(solution)/shard_map/ppermute | solution.py:31
  247.8 6.8 %collective-permute-start.9 = (f32[8,65,128]{2,1,0:T(8,128)S(1)}, f32[8,65,128]{2,1,0:T(8,128)S(1)}, u32[]{:S(2)}, u32[]{:S(2)}) collective-permute-start(f32[8,65,128]{2,1,0:T(8,128)S(1)} %bitcast_subtract_fusion), channel_id=1, source_target_pairs={{4,0},{8,4},{12,8},{16,12},{20,16},{24,20},{28,24},{0,28},{5,1},{9... | collective-permute-start | bytes 798728 | tf_op jit(solution)/shard_map/ppermute | solution.py:31
  256.7 3.6 collective-permute-start.10
  258.3 4.2 %collective-permute-start.11 = (f32[1,65,128]{2,1,0:T(8,128)}, f32[1,65,128]{2,1,0:T(8,128)}, u32[]{:S(2)}, u32[]{:S(2)}) collective-permute-start(f32[1,65,128]{2,1,0:T(8,128)} %get-tuple-element.507), channel_id=1, source_target_pairs={{0,1},{1,2},{2,3},{3,0},{4,5},{5,6},{6,7},{7,4},{8,9},{9,10},{10,1... | collective-permute-start | bytes 99848 | tf_op jit(solution)/shard_map/ppermute | solution.py:22
  264.3 1.7 collective-permute-start.12
  264.3 3.6 collective-permute-start.13
  265.0 3.0 copy-start.12
  265.0 2.9 copy-start.14
  268.6 1.7 collective-permute-start.14
  268.7 3.6 collective-permute-start.15
  269.3 2.9 copy-start.8
  269.3 2.9 copy-start.10
  273.0 1.7 collective-permute-start.16
  273.0 3.6 collective-permute-start.17
  273.7 2.9 copy-start.4
  273.7 2.9 copy-start.6
  319.2 1.8 collective-permute-start.18
  319.4 4.3 %collective-permute-start.19 = (f32[1,65,128]{2,1,0:T(8,128)S(1)}, f32[1,65,128]{2,1,0:T(8,128)S(1)}, u32[]{:S(2)}, u32[]{:S(2)}) collective-permute-start(f32[1,65,128]{2,1,0:T(8,128)S(1)} %get-tuple-element.479), channel_id=1, source_target_pairs={{0,1},{1,2},{2,3},{3,0},{4,5},{5,6},{6,7},{7,4},{8,9},{9,10},{10,1... | collective-permute-start | bytes 99848 | tf_op jit(solution)/shard_map/ppermute | solution.py:22
  324.5 1.7 collective-permute-start.20
  324.6 3.6 collective-permute-start.21
  329.0 1.7 collective-permute-start.22
  329.1 3.6 collective-permute-start.23
  333.5 1.7 collective-permute-start.24
  333.6 3.6 collective-permute-start.25
  337.2 0.7 copy-start.15
  337.9 11.8 %collective-permute-start.26 = (f32[8,65,128]{2,1,0:T(8,128)S(1)}, f32[8,65,128]{2,1,0:T(8,128)S(1)}, u32[]{:S(2)}, u32[]{:S(2)}) collective-permute-start(f32[8,65,128]{2,1,0:T(8,128)S(1)} %convolution_bitcast_fusion.4), channel_id=1, source_target_pairs={{28,0},{0,4},{4,8},{8,12},{12,16},{16,20},{20,24},{24,28},{29,1},{... | collective-permute-start | bytes 798728 | tf_op jit(solution)/shard_map/ppermute | solution.py:31
  349.7 8.2 %collective-permute-start.27 = (f32[8,65,128]{2,1,0:T(8,128)S(1)}, f32[8,65,128]{2,1,0:T(8,128)S(1)}, u32[]{:S(2)}, u32[]{:S(2)}) collective-permute-start(f32[8,65,128]{2,1,0:T(8,128)S(1)} %sub.738), channel_id=1, source_target_pairs={{4,0},{8,4},{12,8},{16,12},{20,16},{24,20},{28,24},{0,28},{5,1},{9... | collective-permute-start | bytes 798728 | tf_op jit(solution)/shard_map/ppermute | solution.py:31
  360.0 2.6 collective-permute-start.28
  360.0 3.7 collective-permute-start.29
  361.9 1.9 copy-start.2
  361.9 1.9 copy-start.16
  365.2 2.1 collective-permute-start.30
  365.6 3.4 collective-permute-start.31
  369.6 2.0 collective-permute-start.32
  370.0 3.4 collective-permute-start.33
  374.1 1.9 collective-permute-start.34
  374.3 3.4 collective-permute-start.35
where the time goes:
time: 423 us; the launch traced here: 420 us
  loops' own time  120 us (28%)
  other arithmetic  85.2 us (20%)
  blocking collectives  79.3 us (19%)
  waiting for transfers between devices  75.2 us (18%)
  local copies, waits for them, and re-layouts  23.4 us (6%)
  starting transfers between devices  18.6 us (4%)
  matrix products  12.9 us (3%)
  between operations  5.19 us (1%)
    another operation x2, loops' own time, inverses(): lax.linalg.tridiagonal_solve(lower[None], centre[None], upper[None], iden...  120 us
    psum x2, blocking collectives, per_device(): lax.psum((0.5 * jnp.sum(mismatch * mismatch), jnp.sum(descent * descent))...  79.3 us
    while x62, other arithmetic  77.8 us
    ppermute x4, waiting for transfers between devices, shifted(): return lax.ppermute(block, axis, route)  31.9 us
    ppermute x16, waiting for transfers between devices, padded_2(): before = lax.ppermute(last, axis, up)  28.1 us
    ppermute x16, waiting for transfers between devices, padded_2(): after = lax.ppermute(initial, axis, down)  15.2 us
    slice x20, local copies, waits for them, and re-layouts, inverses(): lax.linalg.tridiagonal_solve(lower[None], centre[None], upper[None], iden...  11.7 us
    ppermute x16, starting transfers between devices, padded_2(): after = lax.ppermute(initial, axis, down)  8.5 us
  transfers between devices with their start and end apart: 36, of which 33 were waited for; matrix products, arithmetic and copies ran while one was open for 24% of the time, Pallas kernels for 0%

commit v1 on v0

--- a/solution.py
+++ b/solution.py
@@ -2,6 +2,7 @@
 import jax.numpy as jnp
 from jax import lax
 from jax.sharding import PartitionSpec as P
+from jax.lax import psum
 
 NY = 65
 STEPS = 4
@@ -10,6 +11,10 @@
 SPREAD = 0.2
 PUSHED = 0.25
 EPSILON = 1e-06
+
+
+def play_the_paths(local, bus_axis, axis_id):
+    return psum(psum(local, axis_name=bus_axis), axis_name=axis_id)
 
 
 def padded_2(shard, sides, width):
@@ -100,8 +105,10 @@
         mismatch = shifted(earlier, "seg", -1)
         back = adjoint(mismatch, saved, base, inverse)
         descent = back - earlier
-        total, squares = lax.psum(
-            (0.5 * jnp.sum(mismatch * mismatch), jnp.sum(descent * descent)), ("seg", "space")
+        total, squares = play_the_paths(
+            (0.5 * jnp.sum(mismatch * mismatch), jnp.sum(descent * descent)),
+            bus_axis="space",
+            axis_id="seg",
         )
         current = current - total / (squares + EPSILON) * descent
     return (current[None], mismatch[None])

time: 423 us -> 398 us (0.941)
  blocking collectives: 79.3 us -> 55.6 us
    psum x2 -> x4, blocking collectives: 79.3 us -> 55.6 us  [play_the_paths(): return psum(psum(local, axis_name=bus_axis), axis_name=axis_id)]
  transfers between devices with their start and end apart: 36 -> 36, of which waited for: 33 -> 33; matrix products, arithmetic and copies ran while one was open for 24% -> 25% of each run, Pallas kernels for 0% -> 0%
where the time goes in v1:
time: 398 us; the launch traced here: 395 us
  loops' own time  120 us (30%)
  other arithmetic  84.6 us (21%)
  waiting for transfers between devices  76.5 us (19%)
  blocking collectives  55.6 us (14%)
  local copies, waits for them, and re-layouts  23.5 us (6%)
  starting transfers between devices  16.7 us (4%)
  matrix products  12.8 us (3%)
  between operations  5.26 us (1%)
    another operation x2, loops' own time, inverses(): lax.linalg.tridiagonal_solve(lower[None], centre[None], upper[None], iden...  120 us
    while x62, other arithmetic  77.4 us
    psum x4, blocking collectives, play_the_paths(): return psum(psum(local, axis_name=bus_axis), axis_name=axis_id)  55.6 us
    ppermute x4, waiting for transfers between devices, shifted(): return lax.ppermute(block, axis, route)  33.8 us
    ppermute x16, waiting for transfers between devices, padded_2(): before = lax.ppermute(last, axis, up)  27.8 us
    ppermute x16, waiting for transfers between devices, padded_2(): after = lax.ppermute(initial, axis, down)  14.9 us
    slice x20, local copies, waits for them, and re-layouts, inverses(): lax.linalg.tridiagonal_solve(lower[None], centre[None], upper[None], iden...  11.7 us
    ppermute x16, starting transfers between devices, padded_2(): after = lax.ppermute(initial, axis, down)  8.4 us
  transfers between devices with their start and end apart: 36, of which 33 were waited for; matrix products, arithmetic and copies ran while one was open for 25% of the time, Pallas kernels for 0%

profile of v1, /device:TPU:0, one launch (start us, length us, event | category | flops | bytes accessed | tf_op | source)
XLA Modules:
  0.0 395.2 jit_solution(7154879211111134166)
XLA Ops:
  0.6 1.0 copy.69
  1.7 2.5 collective-permute-start
  5.8 169.7 %while.32 = (s32[]{:T(128)}, f32[1]{0:T(128)}, f32[1,65]{1,0:T(1,128)S(1)}, f32[2,32,1]{1,2,0:T(1,128)S(1)}, f32[2,32,1,65]{3,1,2,0:T(8,128)S(1)}, /*index=5*/f3...) while((s32[]{:T(128)}, f32[1]{0:T(128)}, ...), condition=%wide.region_1.2_spmd, body=%wide.region_0.1_spmd.sunk | while | flops 6369 | bytes 103045 | solution.py:47
  7.9 0.7 fusion.724
  8.6 0.7 fusion.726
  10.0 0.7 fusion.725
  92.8 0.7 fusion.724
  93.5 0.7 fusion.726
  94.9 0.7 fusion.725
  175.5 43.9 %while.33 = (s32[]{:T(128)}, f32[1,65]{1,0:T(1,128)S(1)}, f32[2,32,1,65]{3,1,2,0:T(8,128)S(1)}, f32[2,32,1,65]{3,2,1,0:T(1,128)S(1)}, f32[2,32,1]{1,2,0:T(1,128)...) while((s32[]{:T(128)}, f32[1,65]{1,0:T(1,128)S(1)}, ...), condition=%wide.region_3.4_spmd, body=%wide.region_2.3_spmd.sunk | while | flops 4193 | bytes 91485 | solution.py:47
  176.2 0.7 fusion.729
  176.9 19.5 %constant_dynamic-update-slice_fusion.168 = (f32[32,1,65]{2,1,0:T(1,128)S(1)}, f32[1,65]{1,0:T(1,128)S(1)}, f32[1,65]{1,0:T(1,128)S(1)}, f32[1,65]{1,0:T(1,128)S...) fusion(f32[]{:T(128)} %bitcast.1400, ...), kind=kLoop, calls=%fused_computation.196.clone.1 | loop fusion | flops 4029 | bytes 24956 | tf_op jit(solution)/shard_map/vmap()/while
  198.2 0.7 fusion.729
  198.9 19.5 %constant_dynamic-update-slice_fusion.168 = (f32[32,1,65]{2,1,0:T(1,128)S(1)}, f32[1,65]{1,0:T(1,128)S(1)}, f32[1,65]{1,0:T(1,128)S(1)}, f32[1,65]{1,0:T(1,128)S...) fusion(f32[]{:T(128)} %bitcast.1400, ...), kind=kLoop, calls=%fused_computation.196.clone.1 | loop fusion | flops 4029 | bytes 24956 | tf_op jit(solution)/shard_map/vmap()/while
  220.3 1.8 collective-permute-start.2
  222.2 1.7 collective-permute-done.2
  223.9 1.6 collective-permute-done.3
  227.2 1.5 collective-permute-done.4
  228.7 1.7 collective-permute-done.5
  232.0 1.3 collective-permute-done.6
  233.3 1.9 collective-permute-done.7
  235.2 1.5 convolution_bitcast_fusion.12
  236.7 1.5 collective-permute-start.8
  238.2 8.9 %collective-permute-done.8 = f32[8,65,128]{2,1,0:T(8,128)S(1)} collective-permute-done((f32[8,65,128]{2,1,0:T(8,128)S(1)}, f32[8,65,128]{2,1,0:T(8,128)S(1)}, u32[]{:S(2)}, u32[]{:S(2)}) %collective-permute-start.8) | collective-permute-done | bytes 266272 | tf_op jit(solution)/shard_map/ppermute | solution.py:36
  247.2 1.8 collective-permute-start.9
  248.9 5.0 %collective-permute-done.9 = f32[8,65,128]{2,1,0:T(8,128)S(1)} collective-permute-done((f32[8,65,128]{2,1,0:T(8,128)S(1)}, f32[8,65,128]{2,1,0:T(8,128)S(1)}, u32[]{:S(2)}, u32[]{:S(2)}) %collective-permute-start.9) | collective-permute-done | bytes 266272 | tf_op jit(solution)/shard_map/ppermute | solution.py:36
  254.6 0.9 fusion.694
  256.1 1.6 collective-permute-start.10
  257.7 0.7 multiply_reduce_fusion.3
  259.7 2.2 collective-permute-done.11
  261.9 1.7 add_multiply_fusion.5
  264.5 0.8 collective-permute-done.12
  265.3 2.0 collective-permute-done.13
  268.9 0.8 collective-permute-done.14
  269.7 2.0 collective-permute-done.15
  273.2 0.8 collective-permute-done.16
  274.1 2.0 collective-permute-done.17
  276.0 0.9 multiply_reduce_fusion.2
  276.9 6.4 %all-reduce.3 = (f32[]{:T(128)}, f32[]{:T(128)}) all-reduce(f32[]{:T(128)S(6)} %mul.1494, f32[]{:T(128)} %get-tuple-element.308), channel_id=1, replica_groups=mesh['seg'=8,'space'=4] {'space'}, use_global_device_ids=true, to_apply=%region_5.6 | all-reduce | flops 2 | bytes 16 | tf_op jit(solution)/shard_map/psum | solution.py:17
  283.3 22.0 %all-reduce.1 = (f32[]{:T(128)}, f32[]{:T(128)}) all-reduce(f32[]{:T(128)} %get-tuple-element.210, f32[]{:T(128)} %get-tuple-element.211), channel_id=1, replica_groups=mesh['seg'=8,'space'=4] {'seg'}, use_global_device_ids=true, to_apply=%region_6.7 | all-reduce | flops 2 | bytes 16 | tf_op jit(solution)/shard_map/psum | solution.py:17
  307.6 1.0 collective-permute-done.18
  308.6 2.3 collective-permute-done.19
  312.5 1.0 collective-permute-done.20
  313.4 2.0 collective-permute-done.21
  317.0 1.0 collective-permute-done.22
  318.0 2.0 collective-permute-done.23
  321.5 1.0 collective-permute-done.24
  322.5 2.0 collective-permute-done.25
  325.2 11.7 %collective-permute-done.26 = f32[8,65,128]{2,1,0:T(8,128)S(1)} collective-permute-done((f32[8,65,128]{2,1,0:T(8,128)S(1)}, f32[8,65,128]{2,1,0:T(8,128)S(1)}, u32[]{:S(2)}, u32[]{:S(2)}) %collective-permute-start.26) | collective-permute-done | bytes 266272 | tf_op jit(solution)/shard_map/ppermute | solution.py:36
  337.1 8.2 %collective-permute-done.27 = f32[8,65,128]{2,1,0:T(8,128)S(1)} collective-permute-done((f32[8,65,128]{2,1,0:T(8,128)S(1)}, f32[8,65,128]{2,1,0:T(8,128)S(1)}, u32[]{:S(2)}, u32[]{:S(2)}) %collective-permute-start.27) | collective-permute-done | bytes 266272 | tf_op jit(solution)/shard_map/ppermute | solution.py:36
  345.9 0.9 fusion.670
  349.2 0.8 copy.22
  350.0 1.1 collective-permute-done.29
  351.1 1.4 add_multiply_fusion.1
  353.4 1.2 collective-permute-done.30
  354.6 1.7 collective-permute-done.31
  357.8 1.2 collective-permute-done.32
  359.0 1.7 collective-permute-done.33
  362.3 1.1 collective-permute-done.34
  363.3 1.7 collective-permute-done.35
  365.1 0.9 multiply_reduce_fusion
  366.0 6.5 %all-reduce.2 = (f32[]{:T(128)}, f32[]{:T(128)}) all-reduce(f32[]{:T(128)S(6)} %mul.1544, f32[]{:T(128)} %get-tuple-element.306), channel_id=1, replica_groups=mesh['seg'=8,'space'=4] {'space'}, use_global_device_ids=true, to_apply=%region_11.12 | all-reduce | flops 2 | bytes 16 | tf_op jit(solution)/shard_map/psum | solution.py:17
  372.5 20.7 %all-reduce = (f32[]{:T(128)}, f32[]{:T(128)}) all-reduce(f32[]{:T(128)} %get-tuple-element.208, f32[]{:T(128)} %get-tuple-element.209), channel_id=1, replica_groups=mesh['seg'=8,'space'=4] {'seg'}, use_global_device_ids=true, to_apply=%region_12.13 | all-reduce | flops 2 | bytes 16 | tf_op jit(solution)/shard_map/psum | solution.py:17
  394.4 0.8 copy.21
  (303 shorter events, 72.7 us)
Async XLA Ops:
  1.7 217.7 %collective-permute-start = (f32[1,65,128]{2,1,0:T(8,128)S(1)}, f32[1,65,128]{2,1,0:T(8,128)S(1)}, u32[]{:S(2)}, u32[]{:S(2)}) collective-permute-start(f32[1,65,128]{2,1,0:T(8,128)S(1)} %get-tuple-element.530), channel_id=1, source_target_pairs={{1,0},{2,1},{3,2},{0,3},{5,4},{6,5},{7,6},{4,7},{9,8},{10,9},{11,1... | collective-permute-start | bytes 99848 | tf_op jit(solution)/shard_map/ppermute | solution.py:28
  4.1 215.3 %collective-permute-start.1 = (f32[1,65,128]{2,1,0:T(8,128)S(1)}, f32[1,65,128]{2,1,0:T(8,128)S(1)}, u32[]{:S(2)}, u32[]{:S(2)}) collective-permute-start(f32[1,65,128]{2,1,0:T(8,128)S(1)} %get-tuple-element.531), channel_id=1, source_target_pairs={{0,1},{1,2},{2,3},{3,0},{4,5},{5,6},{6,7},{7,4},{8,9},{9,10},{10,1... | collective-permute-start | bytes 99848 | tf_op jit(solution)/shard_map/ppermute | solution.py:27
  4.3 0.7 copy-start.17
  175.5 44.0 %copy-start = (f32[8,65,128]{2,0,1:T(8,128)S(1)}, f32[8,65,128]{2,0,1:T(8,128)}, u32[]{:S(2)}) copy-start(f32[8,65,128]{2,0,1:T(8,128)} %param.8) | copy-start | bytes 798724
  219.4 0.7 copy-start.3
  219.4 0.7 copy-start.5
  220.3 3.6 collective-permute-start.2
  222.1 3.4 collective-permute-start.3
  223.9 2.3 copy-start.7
  225.5 0.7 copy-start.9
  226.3 2.4 collective-permute-start.4
  227.0 3.4 collective-permute-start.5
  228.7 2.4 copy-start.11
  230.4 0.7 copy-start.13
  231.3 2.0 collective-permute-start.6
  231.7 3.5 collective-permute-start.7
  235.2 11.9 %copy-start.1 = (f32[1,8,65,128]{3,1,2,0:T(8,128)S(1)}, f32[1,8,65,128]{3,1,2,0:T(8,128)}, u32[]{:S(2)}) copy-start(f32[1,8,65,128]{3,1,2,0:T(8,128)} %param.7) | copy-start | bytes 798724
  236.7 10.4 %collective-permute-start.8 = (f32[8,65,128]{2,1,0:T(8,128)S(1)}, f32[8,65,128]{2,1,0:T(8,128)S(1)}, u32[]{:S(2)}, u32[]{:S(2)}) collective-permute-start(f32[8,65,128]{2,1,0:T(8,128)S(1)} %convolution_bitcast_fusion.12), channel_id=1, source_target_pairs={{28,0},{0,4},{4,8},{8,12},{12,16},{16,20},{20,24},{24,28},{29,1},{... | collective-permute-start | bytes 798728 | tf_op jit(solution)/shard_map/ppermute | solution.py:36
  247.2 6.8 %collective-permute-start.9 = (f32[8,65,128]{2,1,0:T(8,128)S(1)}, f32[8,65,128]{2,1,0:T(8,128)S(1)}, u32[]{:S(2)}, u32[]{:S(2)}) collective-permute-start(f32[8,65,128]{2,1,0:T(8,128)S(1)} %bitcast_subtract_fusion), channel_id=1, source_target_pairs={{4,0},{8,4},{12,8},{16,12},{20,16},{24,20},{28,24},{0,28},{5,1},{9... | collective-permute-start | bytes 798728 | tf_op jit(solution)/shard_map/ppermute | solution.py:36
  256.1 3.6 collective-permute-start.10
  257.7 4.2 %collective-permute-start.11 = (f32[1,65,128]{2,1,0:T(8,128)}, f32[1,65,128]{2,1,0:T(8,128)}, u32[]{:S(2)}, u32[]{:S(2)}) collective-permute-start(f32[1,65,128]{2,1,0:T(8,128)} %get-tuple-element.511), channel_id=1, source_target_pairs={{0,1},{1,2},{2,3},{3,0},{4,5},{5,6},{6,7},{7,4},{8,9},{9,10},{10,1... | collective-permute-start | bytes 99848 | tf_op jit(solution)/shard_map/ppermute | solution.py:27
  263.6 1.7 collective-permute-start.12
  263.7 3.6 collective-permute-start.13
  264.4 3.0 copy-start.12
  264.4 3.0 copy-start.14
  268.0 1.7 collective-permute-start.14
  268.1 3.6 collective-permute-start.15
  268.7 2.9 copy-start.8
  268.7 2.9 copy-start.10
  272.4 1.7 collective-permute-start.16
  272.4 3.6 collective-permute-start.17
  273.1 2.9 copy-start.4
  273.1 2.9 copy-start.6
  306.9 1.7 collective-permute-start.18
  307.0 3.9 collective-permute-start.19
  311.8 1.7 collective-permute-start.20
  311.8 3.7 collective-permute-start.21
  316.3 1.7 collective-permute-start.22
  316.4 3.6 collective-permute-start.23
  320.8 1.7 collective-permute-start.24
  320.9 3.6 collective-permute-start.25
  324.5 0.7 copy-start.15
  325.2 11.8 %collective-permute-start.26 = (f32[8,65,128]{2,1,0:T(8,128)S(1)}, f32[8,65,128]{2,1,0:T(8,128)S(1)}, u32[]{:S(2)}, u32[]{:S(2)}) collective-permute-start(f32[8,65,128]{2,1,0:T(8,128)S(1)} %convolution_bitcast_fusion.4), channel_id=1, source_target_pairs={{28,0},{0,4},{4,8},{8,12},{12,16},{16,20},{20,24},{24,28},{29,1},{... | collective-permute-start | bytes 798728 | tf_op jit(solution)/shard_map/ppermute | solution.py:36
  337.0 8.3 %collective-permute-start.27 = (f32[8,65,128]{2,1,0:T(8,128)S(1)}, f32[8,65,128]{2,1,0:T(8,128)S(1)}, u32[]{:S(2)}, u32[]{:S(2)}) collective-permute-start(f32[8,65,128]{2,1,0:T(8,128)S(1)} %sub.738), channel_id=1, source_target_pairs={{4,0},{8,4},{12,8},{16,12},{20,16},{24,20},{28,24},{0,28},{5,1},{9... | collective-permute-start | bytes 798728 | tf_op jit(solution)/shard_map/ppermute | solution.py:36
  347.4 2.6 collective-permute-start.28
  347.4 3.7 collective-permute-start.29
  349.2 1.9 copy-start.2
  349.2 1.9 copy-start.16
  352.5 2.1 collective-permute-start.30
  352.9 3.4 collective-permute-start.31
  357.0 2.0 collective-permute-start.32
  357.4 3.4 collective-permute-start.33
  361.4 1.9 collective-permute-start.34
  361.7 3.4 collective-permute-start.35
